TPU v7x, 32 devices: a whole 2x2x4 slice. The times are simulated.
32 devices in a mesh: groups: 2 (over y), space: 8 (over z, x), dp: 2 (over core).
Axes of the slice: x: 2, y: 2, z: 4, core: 2. Of those that a mesh axis runs over, the one named last changes fastest.
Arguments:
- features: bfloat16 [4, 16, 8, 8, 512], P(('groups', 'dp'), 'space'), parts along dimension 0, may hold values from -6 to 6
- cotangent: bfloat16 [4, 16, 8, 8, 512], P(('groups', 'dp'), 'space'), parts along dimension 0, may hold values from -6 to 6
- kernel: bfloat16 [3, 3, 3, 64, 64], replicated, may hold values from -0.15625 to 0.15625
- neighbours: int32 [4, 16, 6], P(('groups', 'dp'), 'space'), parts along dimension 0, may hold values from -1 to 15, as said below
Outputs:
- response: bfloat16 [4, 16, 8, 8, 512], P(('groups', 'dp'), 'space'), parts along dimension 0
- feature_grad: bfloat16 [4, 16, 8, 8, 512], P(('groups', 'dp'), 'space'), parts along dimension 0
- kernel_grad: float32 [6, 3, 3, 64, 64], P('groups'), parts along dimension 0
There are 2 independent parts, one for each index of `groups`. A program takes and returns all parts, laid end to end along the dimension named above; an argument that names none is the same for every part. Nothing has to cross between parts.
Inputs may be any that keep to these rules, and one draw needn't show every extreme that they name: `neighbours`: the active bricks lie on a lattice of 3 by 8 by 4 bricks. Tile t sits at position p = t + 2: it covers lattice row p // 4 of the first dimension, rows 2 * (p % 4) to 2 * (p % 4) + 1 of the second and all rows of the third; it holds exactly 2 active bricks, in slots 2 * t to 2 * t + 1, listed by second then third lattice coordinate. In each realization one third-dimension row z is drawn, and every tile holds the bricks at z in its first and in its last second-dimension row; its other bricks are drawn at random. Directions are first dimension down, up, second down, up, third down, up; the relation is symmetric (if brick u is the up neighbour of s, s is the down neighbour of u), and -1 marks a neighbour that is inactive or outside the lattice.
All inputs are finite; a program needn't handle non-finite values.
Results may differ from a plain program's by a relative error of at most 0.0045.
Values may be sent and summed in bfloat16 or wider, within the bound.
No kernel may reach another device: no remote copies, remote signals or barrier semaphores. Data moves between devices by JAX's collectives and lax.ppermute only.
A program may use at most 64 MiB of HBM per device.

v0:
```python
import math
import jax
import jax.numpy as jnp
from jax import lax
from jax.sharding import PartitionSpec as P

TILES_Y = 4


def shifted(x, axis, by):
    count = lax.axis_size(axis)
    pairs = [(i, i + by) for i in range(count) if 0 <= i + by < count]
    return lax.ppermute(x, axis, pairs)


def choose_rows(tables, shifts, column, source_device, flat_slot, present, position):
    stacked = jnp.concatenate(tables, axis=0)
    row_count = tables[0].shape[0]
    source_pick = jnp.zeros_like(flat_slot[:, column])
    for number, offset in enumerate(shifts):
        source_pick = jnp.where(source_device[:, column] == position + offset, number, source_pick)
    row_index = source_pick * row_count + flat_slot[:, column]
    picked = jnp.take(stacked, row_index, axis=0)
    present_rows = present[:, column].reshape((-1,) + (1,) * (picked.ndim - 1))
    return jnp.where(present_rows, picked, jnp.zeros_like(picked))


def make_banded(weights, channels):
    toeplitz = jnp.zeros((3, 3, 4, channels, 2, channels), jnp.bfloat16)
    for out_cell in range(2):
        for tap_z in range(3):
            toeplitz = toeplitz.at[:, :, out_cell + tap_z, :, out_cell, :].set(weights[:, :, tap_z])
    return toeplitz.reshape(3, 3, 4 * channels, 2 * channels)


def make_windows(extended, channels, pairs_z):
    return jnp.stack(
        [
            extended[..., 2 * channels * block_index : 2 * channels * block_index + 4 * channels]
            for block_index in range(pairs_z)
        ],
        axis=3,
    )


def correlate(windows, banded, rows_all, brick_edge, pairs_z, channels):
    result = jnp.zeros((rows_all, brick_edge, brick_edge, pairs_z, 2 * channels), jnp.float32)
    for row_offset in range(3):
        for col_offset in range(3):
            window_part = windows[
                :, row_offset : row_offset + brick_edge, col_offset : col_offset + brick_edge
            ]
            result = result + jnp.einsum(
                "nabjk,kc->nabjc",
                window_part,
                banded[row_offset, col_offset],
                preferred_element_type=jnp.float32,
            )
    return result


def body(features, cotangent, kernel, neighbours):
    realizations = features.shape[0]
    bricks = features.shape[1]
    brick_edge = features.shape[2]
    channels = kernel.shape[-1]
    rows_all = realizations * bricks
    tile_stride = TILES_Y
    pairs_z = brick_edge // 2
    position = lax.axis_index("space")
    neighbour_slots = neighbours.reshape(rows_all, 6)
    present = neighbour_slots >= 0
    safe_links = jnp.where(present, neighbour_slots, 0)
    source_device = safe_links // bricks
    base_rows = jnp.repeat(jnp.arange(realizations, dtype=jnp.int32) * bricks, bricks)[:, None]
    flat_slot = base_rows + safe_links % bricks

    def select(tables, shifts, column):
        return choose_rows(tables, shifts, column, source_device, flat_slot, present, position)

    volume = features.reshape(rows_all, brick_edge, brick_edge, brick_edge * channels)
    upper_face = volume[:, brick_edge - 1]
    lower_face = volume[:, 0]
    from_below = shifted(upper_face, "space", tile_stride)
    from_above = shifted(lower_face, "space", -tile_stride)
    below_part = select([upper_face, from_below], [0, -tile_stride], 0)
    above_part = select([lower_face, from_above], [0, tile_stride], 1)
    layered_x = jnp.concatenate([below_part[:, None], volume, above_part[:, None]], axis=1)
    upper_face = layered_x[:, :, brick_edge - 1]
    lower_face = layered_x[:, :, 0]
    from_below = shifted(upper_face, "space", 1)
    from_above = shifted(lower_face, "space", -1)
    below_part = select([upper_face, from_below], [0, -1], 2)
    above_part = select([lower_face, from_above], [0, 1], 3)
    layered_y = jnp.concatenate([below_part[:, :, None], layered_x, above_part[:, :, None]], axis=2)
    upper_face = layered_y[..., (brick_edge - 1) * channels :]
    lower_face = layered_y[..., :channels]
    extended = jnp.concatenate(
        [select([upper_face], [0], 4), layered_y, select([lower_face], [0], 5)], axis=-1
    )
    banded = make_banded(kernel, channels)
    windows = make_windows(extended, channels, pairs_z)
    result = correlate(windows, banded, rows_all, brick_edge, pairs_z, channels)
    response = result.reshape(features.shape).astype(jnp.bfloat16)
    cotangent_pairs = cotangent.reshape(rows_all, brick_edge, brick_edge, pairs_z, 2 * channels)
    band_terms = []
    for row_offset in range(3):
        for col_offset in range(3):
            window_part = windows[
                :, row_offset : row_offset + brick_edge, col_offset : col_offset + brick_edge
            ]
            band_terms.append(
                jnp.einsum(
                    "nabjk,nabjc->kc",
                    window_part,
                    cotangent_pairs,
                    preferred_element_type=jnp.float32,
                )
            )
    band_grad = jnp.stack(band_terms).reshape(3, 3, 4, channels, 2, channels)
    kernel_local = jnp.stack(
        [
            band_grad[:, :, tap_z, :, 0, :] + band_grad[:, :, tap_z + 1, :, 1, :]
            for tap_z in range(3)
        ],
        axis=2,
    )
    cells_all = rows_all * lax.axis_size("dp") * lax.axis_size("space") * brick_edge**3
    factor = 1.0 / math.sqrt(cells_all)
    kernel_grad = lax.psum(kernel_local, ("space", "dp")) * factor
    spread = jnp.zeros(
        (rows_all, brick_edge + 2, brick_edge + 2, pairs_z, 4 * channels), jnp.float32
    )
    for row_offset in range(3):
        for col_offset in range(3):
            contribution = jnp.einsum(
                "nabjc,kc->nabjk",
                cotangent_pairs,
                banded[row_offset, col_offset],
                preferred_element_type=jnp.float32,
            )
            spread = spread.at[
                :, row_offset : row_offset + brick_edge, col_offset : col_offset + brick_edge
            ].add(contribution)
    widened = jnp.zeros(
        (rows_all, brick_edge + 2, brick_edge + 2, (brick_edge + 2) * channels), jnp.float32
    )
    for block_index in range(pairs_z):
        widened = widened.at[
            ..., 2 * channels * block_index : 2 * channels * block_index + 4 * channels
        ].add(spread[..., block_index, :])
    lower_rim = widened[..., :channels]
    upper_rim = widened[..., (brick_edge + 1) * channels :]
    trimmed_z = widened[..., channels : (brick_edge + 1) * channels]
    trimmed_z = trimmed_z.at[..., (brick_edge - 1) * channels :].add(select([lower_rim], [0], 5))
    trimmed_z = trimmed_z.at[..., :channels].add(select([upper_rim], [0], 4))
    lower_rim = trimmed_z[:, :, 0]
    upper_rim = trimmed_z[:, :, brick_edge + 1]
    trimmed_y = trimmed_z[:, :, 1 : brick_edge + 1]
    from_below = shifted(upper_rim.astype(jnp.bfloat16), "space", 1).astype(upper_rim.dtype)
    from_above = shifted(lower_rim.astype(jnp.bfloat16), "space", -1).astype(lower_rim.dtype)
    trimmed_y = trimmed_y.at[:, :, brick_edge - 1].add(select([lower_rim, from_above], [0, 1], 3))
    trimmed_y = trimmed_y.at[:, :, 0].add(select([upper_rim, from_below], [0, -1], 2))
    lower_rim = trimmed_y[:, 0]
    upper_rim = trimmed_y[:, brick_edge + 1]
    trimmed_x = trimmed_y[:, 1 : brick_edge + 1]
    from_below = shifted(upper_rim.astype(jnp.bfloat16), "space", tile_stride).astype(
        upper_rim.dtype
    )
    from_above = shifted(lower_rim.astype(jnp.bfloat16), "space", -tile_stride).astype(
        lower_rim.dtype
    )
    trimmed_x = trimmed_x.at[:, brick_edge - 1].add(
        select([lower_rim, from_above], [0, tile_stride], 1)
    )
    trimmed_x = trimmed_x.at[:, 0].add(select([upper_rim, from_below], [0, -tile_stride], 0))
    feature_grad = trimmed_x.reshape(features.shape).astype(jnp.bfloat16)
    return (response, feature_grad, kernel_grad)


def solution(mesh):
    in_specs = (
        P(("groups", "dp"), "space", None, None, None),
        P(("groups", "dp"), "space", None, None, None),
        P(),
        P(("groups", "dp"), "space", None),
    )
    out_specs = (
        P(("groups", "dp"), "space", None, None, None),
        P(("groups", "dp"), "space", None, None, None),
        P("groups", None, None, None, None),
    )
    return jax.shard_map(body, mesh=mesh, in_specs=in_specs, out_specs=out_specs, check_vma=False)
```

profile of v0, /device:TPU:0, one launch (start us, length us, event | category | flops | bytes accessed | tf_op | source)
XLA Modules:
  0.0 196.4 jit_solution(7922815339144183871)
XLA Ops:
  8.0 5.9 %collective-permute-start = (bf16[2,8,512]{2,1,0:T(8,128)(2,1)S(1)}, bf16[2,8,512]{2,1,0:T(8,128)(2,1)S(1)}, u32[]{:S(2)}, u32[]{:S(2)}) collective-permute-start(bf16[2,8,512]{2,1,0:T(8,128)(2,1)S(1)} %get-tuple-element.377), channel_id=1, source_target_pairs={{0,8},{2,10},{4,12},{6,14},{1,9},{3,11},{5,13},{7,15},{16,24},{18,... | collective-permute-start | bytes 49160 | tf_op jit(solution)/shard_map/ppermute | solution.py:13
  14.0 1.3 collective-permute-start.1
  19.5 1.2 copy.377
  22.5 1.5 fusion.10
  24.0 2.8 %scatter-add.65 = f32[2,10,10,4,256]{4,2,1,0,3:T(8,128)S(1)} dynamic-update-slice(f32[2,10,10,4,256]{4,2,1,0,3:T(8,128)S(1)} %scatter-add.64, f32[2,8,8,4,256]{4,2,1,0,3:T(8,128)S(1)} %fusion.10, s32[]{:T(128)} %constant.794.clone.1, s32[]{:T(128)} %bitcast.54, s32[]{:T(128)} %bitcast.55, s32[]{:T(128)} %constant.794.clone.1, s32[]{:T(128)} %constant.794.clone.1) | dynamic-update-slice | bytes 1048580 | tf_op jit(solution)/shard_map/scatter-add | solution.py:144
  26.9 2.1 %fusion.9 = f32[2,8,8,4,256]{4,2,1,0,3:T(8,128)S(1)} fusion(f32[2,10,10,4,256]{4,2,1,0,3:T(8,128)S(1)} %scatter-add.65, s32[]{:T(128)} %bitcast.59, s32[]{:T(128)} %bitcast.60, pred[]{:T(512)} %and_reduce_fusion, bf16[3,3,256,128]{3,2,1,0:T(8,128)(2,1)S(1)} %reshape.1187, bf16[1,2,8,8,512]{4,3,2,1,0:T(8,128)(2,1)S(1)} %copy-done), kind=kOutput, calls=%fused_computation.28 | convolution fusion | flops 33816576 | bytes 1245193 | tf_op jit(solution)/shard_map/nabjc,kc->nabjk/dot_general | solution.py:136
  29.0 2.9 %scatter-add.66 = f32[2,10,10,4,256]{4,2,1,0,3:T(8,128)S(1)} dynamic-update-slice(f32[2,10,10,4,256]{4,2,1,0,3:T(8,128)S(1)} %scatter-add.65, f32[2,8,8,4,256]{4,2,1,0,3:T(8,128)S(1)} %fusion.9, s32[]{:T(128)} %constant.794.clone.1, s32[]{:T(128)} %bitcast.59, s32[]{:T(128)} %bitcast.60, s32[]{:T(128)} %constant.794.clone.1, s32[]{:T(128)} %constant.794.clone.1) | dynamic-update-slice | bytes 1048580 | tf_op jit(solution)/shard_map/scatter-add | solution.py:144
  32.4 1.5 scatter-add.70
  34.2 1.5 scatter-add.71
  36.3 1.5 scatter-add.75
  38.0 1.5 scatter-add.76
  41.7 3.1 %scatter-add.85 = f32[2,10,10,512]{3,2,1,0:T(8,128)S(1)} dynamic-update-slice(f32[2,10,10,512]{3,2,1,0:T(8,128)S(1)} %slice.1260, f32[2,10,10,64]{3,2,1,0:T(8,128)S(1)} %get-tuple-element.368, s32[]{:T(128)} %constant.794.clone.1, s32[]{:T(128)} %constant.794.clone.1, s32[]{:T(128)} %constant.794.clone.1, s32[]{:T(128)} %constant.811.clone.1) | dynamic-update-slice | bytes 102404 | tf_op jit(solution)/shard_map/scatter-add | solution.py:155
  45.6 1.3 collective-permute-start.4
  46.9 4.5 %collective-permute-start.5 = (bf16[2,10,512]{2,0,1:T(2,128)(2,1)S(1)}, bf16[2,10,512]{2,0,1:T(2,128)(2,1)S(1)}, u32[]{:S(2)}, u32[]{:S(2)}) collective-permute-start(bf16[2,10,512]{2,0,1:T(2,128)(2,1)S(1)} %bitcast.421), channel_id=1, source_target_pairs={{0,2},{2,4},{4,6},{6,8},{8,10},{10,12},{12,14},{1,3},{3,5},{5,7},{... | collective-permute-start | bytes 61448 | tf_op jit(solution)/shard_map/ppermute | solution.py:13
  53.2 1.3 collective-permute-start.3
  54.5 4.9 %collective-permute-start.2 = (bf16[2,10,512]{2,1,0:T(8,128)(2,1)S(1)}, bf16[2,10,512]{2,1,0:T(8,128)(2,1)S(1)}, u32[]{:S(2)}, u32[]{:S(2)}) collective-permute-start(bf16[2,10,512]{2,1,0:T(8,128)(2,1)S(1)} %copy.364), channel_id=1, source_target_pairs={{0,2},{2,4},{4,6},{6,8},{8,10},{10,12},{12,14},{1,3},{3,5},{5,7},{... | collective-permute-start | bytes 61448 | tf_op jit(solution)/shard_map/ppermute | solution.py:13
  61.4 5.4 %collective-permute-start.7 = (bf16[2,8,512]{2,1,0:T(8,128)(2,1)S(1)}, bf16[2,8,512]{2,1,0:T(8,128)(2,1)S(1)}, u32[]{:S(2)}, u32[]{:S(2)}) collective-permute-start(bf16[2,8,512]{2,1,0:T(8,128)(2,1)S(1)} %get-tuple-element.365), channel_id=1, source_target_pairs={{0,8},{2,10},{4,12},{6,14},{1,9},{3,11},{5,13},{7,15},{16,24},{18,... | collective-permute-start | bytes 49160 | tf_op jit(solution)/shard_map/ppermute | solution.py:13
  66.9 1.5 collective-permute-start.6
  72.3 1.4 fusion.129
  85.9 2.7 %reshape.1202 = f32[3,3,4,64,2,64]{5,4,3,2,1,0:T(2,128)S(1)} reshape(f32[9,256,128]{2,1,0:T(8,128)} %fusion.13) | data formatting | bytes 2359296 | tf_op jit(solution)/shard_map/reshape | solution.py:120
  88.6 1.9 fusion.128
  91.7 1.7 fusion.12
  93.4 94.0 %all-reduce.5.cloned.1.call-done = f32[3,3,3,64,64]{4,3,2,1,0:T(8,128)} async-done(((f32[3,3,3,64,64]{4,3,2,1,0:T(8,128)}), f32[3,3,3,64,64]{4,3,2,1,0:T(8,128)}) %all-reduce.5.cloned.1.call-update) | async-done | bytes 442384 | tf_op jit(solution)/shard_map/psum | solution.py:130
  187.4 2.2 %broadcast_multiply_fusion = f32[3,3,3,64,64]{4,3,2,1,0:T(8,128)} fusion(f32[3,3,3,64,64]{4,3,2,1,0:T(8,128)} %all-reduce.5.cloned.1.call-done), kind=kLoop, calls=%fused_computation.62 | loop fusion | flops 110592 | bytes 884736 | tf_op jit(solution)/shard_map/mul | solution.py:130
  (170 shorter events, 31.5 us)
Async XLA Ops:
  7.2 14.9 %copy-start = (bf16[1,2,8,8,512]{4,3,2,1,0:T(8,128)(2,1)S(1)}, bf16[1,2,8,8,512]{4,3,2,1,0:T(8,128)(2,1)}, u32[]{:S(2)}) copy-start(bf16[1,2,8,8,512]{4,3,2,1,0:T(8,128)(2,1)} %param.67) | copy-start | bytes 393220
  7.2 12.2 %copy-start.2 = (bf16[3,3,3,64,64]{4,3,2,1,0:T(8,128)(2,1)S(1)}, bf16[3,3,3,64,64]{4,3,2,1,0:T(8,128)(2,1)}, u32[]{:S(2)}) copy-start(bf16[3,3,3,64,64]{4,3,2,1,0:T(8,128)(2,1)} %param.68) | copy-start | bytes 663556
  7.2 180.2 %all-reduce.5.cloned.1.call-start = ((), (), s32[]{:S(2)}) async-start(), calls=%async_computation | async-start | bytes 1769472 | tf_op jit(solution)/shard_map/psum | solution.py:130
  8.0 43.7 %collective-permute-start = (bf16[2,8,512]{2,1,0:T(8,128)(2,1)S(1)}, bf16[2,8,512]{2,1,0:T(8,128)(2,1)S(1)}, u32[]{:S(2)}, u32[]{:S(2)}) collective-permute-start(bf16[2,8,512]{2,1,0:T(8,128)(2,1)S(1)} %get-tuple-element.377), channel_id=1, source_target_pairs={{0,8},{2,10},{4,12},{6,14},{1,9},{3,11},{5,13},{7,15},{16,24},{18,... | collective-permute-start | bytes 49160 | tf_op jit(solution)/shard_map/ppermute | solution.py:13
  14.0 38.3 %collective-permute-start.1 = (bf16[2,8,512]{2,1,0:T(8,128)(2,1)S(1)}, bf16[2,8,512]{2,1,0:T(8,128)(2,1)S(1)}, u32[]{:S(2)}, u32[]{:S(2)}) collective-permute-start(bf16[2,8,512]{2,1,0:T(8,128)(2,1)S(1)} %get-tuple-element.378), channel_id=1, source_target_pairs={{8,0},{10,2},{12,4},{14,6},{9,1},{11,3},{13,5},{15,7},{24,16},{26,... | collective-permute-start | bytes 49160 | tf_op jit(solution)/shard_map/ppermute | solution.py:13
  20.7 0.7 copy-start.10
  21.4 53.8 %copy-start.1 = (bf16[3,3,256,128]{3,2,1,0:T(8,128)(2,1)}, bf16[3,3,256,128]{3,2,1,0:T(8,128)(2,1)S(1)}, u32[]{:S(2)}) copy-start(bf16[3,3,256,128]{3,2,1,0:T(8,128)(2,1)S(1)} %reshape.1187) | copy-start | bytes 1769476
  44.9 8.1 %copy-start.3 = (bf16[1,2,8,8,512]{4,3,2,1,0:T(8,128)(2,1)S(1)}, bf16[1,2,8,8,512]{4,3,2,1,0:T(8,128)(2,1)}, u32[]{:S(2)}) copy-start(bf16[1,2,8,8,512]{4,3,2,1,0:T(8,128)(2,1)} %param.66) | copy-start | bytes 393220
  45.6 13.9 %collective-permute-start.4 = (bf16[2,10,512]{2,0,1:T(2,128)(2,1)S(1)}, bf16[2,10,512]{2,0,1:T(2,128)(2,1)S(1)}, u32[]{:S(2)}, u32[]{:S(2)}) collective-permute-start(bf16[2,10,512]{2,0,1:T(2,128)(2,1)S(1)} %bitcast.420), channel_id=1, source_target_pairs={{2,0},{4,2},{6,4},{8,6},{10,8},{12,10},{14,12},{3,1},{5,3},{7,5},{... | collective-permute-start | bytes 61448 | tf_op jit(solution)/shard_map/ppermute | solution.py:13
  46.9 12.5 %collective-permute-start.5 = (bf16[2,10,512]{2,0,1:T(2,128)(2,1)S(1)}, bf16[2,10,512]{2,0,1:T(2,128)(2,1)S(1)}, u32[]{:S(2)}, u32[]{:S(2)}) collective-permute-start(bf16[2,10,512]{2,0,1:T(2,128)(2,1)S(1)} %bitcast.421), channel_id=1, source_target_pairs={{0,2},{2,4},{4,6},{6,8},{8,10},{10,12},{12,14},{1,3},{3,5},{5,7},{... | collective-permute-start | bytes 61448 | tf_op jit(solution)/shard_map/ppermute | solution.py:13
  53.2 15.2 %collective-permute-start.3 = (bf16[2,10,512]{2,1,0:T(8,128)(2,1)S(1)}, bf16[2,10,512]{2,1,0:T(8,128)(2,1)S(1)}, u32[]{:S(2)}, u32[]{:S(2)}) collective-permute-start(bf16[2,10,512]{2,1,0:T(8,128)(2,1)S(1)} %copy.368), channel_id=1, source_target_pairs={{2,0},{4,2},{6,4},{8,6},{10,8},{12,10},{14,12},{3,1},{5,3},{7,5},{... | collective-permute-start | bytes 61448 | tf_op jit(solution)/shard_map/ppermute | solution.py:13
  54.5 14.6 %collective-permute-start.2 = (bf16[2,10,512]{2,1,0:T(8,128)(2,1)S(1)}, bf16[2,10,512]{2,1,0:T(8,128)(2,1)S(1)}, u32[]{:S(2)}, u32[]{:S(2)}) collective-permute-start(bf16[2,10,512]{2,1,0:T(8,128)(2,1)S(1)} %copy.364), channel_id=1, source_target_pairs={{0,2},{2,4},{4,6},{6,8},{8,10},{10,12},{12,14},{1,3},{3,5},{5,7},{... | collective-permute-start | bytes 61448 | tf_op jit(solution)/shard_map/ppermute | solution.py:13
  61.4 14.0 %collective-permute-start.7 = (bf16[2,8,512]{2,1,0:T(8,128)(2,1)S(1)}, bf16[2,8,512]{2,1,0:T(8,128)(2,1)S(1)}, u32[]{:S(2)}, u32[]{:S(2)}) collective-permute-start(bf16[2,8,512]{2,1,0:T(8,128)(2,1)S(1)} %get-tuple-element.365), channel_id=1, source_target_pairs={{0,8},{2,10},{4,12},{6,14},{1,9},{3,11},{5,13},{7,15},{16,24},{18,... | collective-permute-start | bytes 49160 | tf_op jit(solution)/shard_map/ppermute | solution.py:13
  66.9 9.1 %collective-permute-start.6 = (bf16[2,8,512]{2,1,0:T(8,128)(2,1)S(1)}, bf16[2,8,512]{2,1,0:T(8,128)(2,1)S(1)}, u32[]{:S(2)}, u32[]{:S(2)}) collective-permute-start(bf16[2,8,512]{2,1,0:T(8,128)(2,1)S(1)} %get-tuple-element.366), channel_id=1, source_target_pairs={{8,0},{10,2},{12,4},{14,6},{9,1},{11,3},{13,5},{15,7},{24,16},{26,... | collective-permute-start | bytes 49160 | tf_op jit(solution)/shard_map/ppermute | solution.py:13
  75.4 2.1 %copy-start.9 = (bf16[2,8,8,4,256]{4,2,3,1,0:T(8,128)(2,1)S(1)}, bf16[2,8,8,4,256]{4,2,3,1,0:T(8,128)(2,1)}, u32[]{:S(2)}) copy-start(bf16[2,8,8,4,256]{4,2,3,1,0:T(8,128)(2,1)} %get-tuple-element.360) | copy-start | bytes 786436
  77.5 1.0 copy-start.8
  78.4 0.9 copy-start.7
  79.4 0.9 copy-start.6
  80.3 0.9 copy-start.5
  81.3 0.9 copy-start.4
Sparse Core Ops, SparseCore 0:
  91.8 95.5 all-reduce.4
where the time goes:
time: 197 us; the launch traced here: 196 us
  waiting for transfers between devices  94 us (48%)
  local copies, waits for them, and re-layouts  35.9 us (18%)
  starting transfers between devices  26.2 us (13%)
  matrix products  17.3 us (9%)
  between operations  15.1 us (8%)
  other arithmetic  7.91 us (4%)
    psum x1, waiting for transfers between devices, body(): kernel_grad = lax.psum(kernel_local, ('space', 'dp')) * factor  94 us
    ppermute x8, starting transfers between devices, shifted(): return lax.ppermute(x, axis, pairs)  26.2 us
    scatter-add x7, local copies, waits for them, and re-layouts, body(): spread = spread.at[:, row_offset:row_offset + brick_edge, col_offset:col_...  12 us
    dot_general x9, matrix products, body(): jnp.einsum('nabjk,nabjc->kc', window_part, cotangent_pairs, preferred_ele...  8.32 us
    gather x12, local copies, waits for them, and re-layouts, choose_rows(): picked = jnp.take(stacked, row_index, axis=0)  6.66 us
    dot_general x9, matrix products, body(): jnp.einsum('nabjc,kc->nabjk', cotangent_pairs, banded[row_offset, col_off...  5.35 us
  transfers between devices with their start and end apart: 9, of which 1 were waited for; matrix products, arithmetic and copies ran while one was open for 22% of the time, Pallas kernels for 0%

commit v1 on v0

--- a/solution.py
+++ b/solution.py
@@ -127,7 +127,7 @@
     )
     cells_all = rows_all * lax.axis_size("dp") * lax.axis_size("space") * brick_edge**3
     factor = 1.0 / math.sqrt(cells_all)
-    kernel_grad = lax.psum(kernel_local, ("space", "dp")) * factor
+    kernel_grad = lax.psum(lax.psum(kernel_local, "dp"), "space") * factor
     spread = jnp.zeros(
         (rows_all, brick_edge + 2, brick_edge + 2, pairs_z, 4 * channels), jnp.float32
     )

time: 197 us -> 204 us (1.036)
  waiting for transfers between devices: 94 us -> 97.6 us
  matrix products: 17.3 us -> 19.8 us
    psum x1 -> x2, waiting for transfers between devices: 94 us -> 97.6 us  [body(): kernel_grad = lax.psum(lax.psum(kernel_local, 'dp'), 'space') * factor]
    dot_general x9, matrix products: 3.63 us -> 6.15 us  [correlate(): jnp.einsum('nabjk,kc->nabjc', window_part, banded[row_offset, col_offset]...]
  transfers between devices with their start and end apart: 9 -> 10, of which waited for: 1 -> 2; matrix products, arithmetic and copies ran while one was open for 22% -> 22% of each run, Pallas kernels for 0% -> 0%
where the time goes in v1:
time: 204 us; the launch traced here: 203 us
  waiting for transfers between devices  97.6 us (48%)
  local copies, waits for them, and re-layouts  36 us (18%)
  starting transfers between devices  26.3 us (13%)
  matrix products  19.8 us (10%)
  between operations  15.1 us (7%)
  other arithmetic  7.93 us (4%)
    psum x2, waiting for transfers between devices, body(): kernel_grad = lax.psum(lax.psum(kernel_local, 'dp'), 'space') * factor  97.6 us
    ppermute x8, starting transfers between devices, shifted(): return lax.ppermute(x, axis, pairs)  26.2 us
    scatter-add x7, local copies, waits for them, and re-layouts, body(): spread = spread.at[:, row_offset:row_offset + brick_edge, col_offset:col_...  12 us
    dot_general x9, matrix products, body(): jnp.einsum('nabjk,nabjc->kc', window_part, cotangent_pairs, preferred_ele...  8.3 us
    gather x12, local copies, waits for them, and re-layouts, choose_rows(): picked = jnp.take(stacked, row_index, axis=0)  6.66 us
    dot_general x9, matrix products, correlate(): jnp.einsum('nabjk,kc->nabjc', window_part, banded[row_offset, col_offset]...  6.15 us
    dot_general x9, matrix products, body(): jnp.einsum('nabjc,kc->nabjk', cotangent_pairs, banded[row_offset, col_off...  5.34 us
  transfers between devices with their start and end apart: 10, of which 2 were waited for; matrix products, arithmetic and copies ran while one was open for 22% of the time, Pallas kernels for 0%

profile of v1, /device:TPU:0, one launch (start us, length us, event | category | flops | bytes accessed | tf_op | source)
XLA Modules:
  0.0 202.7 jit_solution(7210605704151709471)
XLA Ops:
  8.0 5.9 %collective-permute-start = (bf16[2,8,512]{2,1,0:T(8,128)(2,1)S(1)}, bf16[2,8,512]{2,1,0:T(8,128)(2,1)S(1)}, u32[]{:S(2)}, u32[]{:S(2)}) collective-permute-start(bf16[2,8,512]{2,1,0:T(8,128)(2,1)S(1)} %get-tuple-element.377), channel_id=1, source_target_pairs={{0,8},{2,10},{4,12},{6,14},{1,9},{3,11},{5,13},{7,15},{16,24},{18,... | collective-permute-start | bytes 49160 | tf_op jit(solution)/shard_map/ppermute | solution.py:13
  14.0 1.3 collective-permute-start.1
  22.5 1.5 fusion.10
  24.0 2.8 %scatter-add.65 = f32[2,10,10,4,256]{4,2,1,0,3:T(8,128)S(1)} dynamic-update-slice(f32[2,10,10,4,256]{4,2,1,0,3:T(8,128)S(1)} %scatter-add.64, f32[2,8,8,4,256]{4,2,1,0,3:T(8,128)S(1)} %fusion.10, s32[]{:T(128)} %constant.794.clone.1, s32[]{:T(128)} %bitcast.54, s32[]{:T(128)} %bitcast.55, s32[]{:T(128)} %constant.794.clone.1, s32[]{:T(128)} %constant.794.clone.1) | dynamic-update-slice | bytes 1048580 | tf_op jit(solution)/shard_map/scatter-add | solution.py:144
  26.9 2.1 %fusion.9 = f32[2,8,8,4,256]{4,2,1,0,3:T(8,128)S(1)} fusion(f32[2,10,10,4,256]{4,2,1,0,3:T(8,128)S(1)} %scatter-add.65, s32[]{:T(128)} %bitcast.59, s32[]{:T(128)} %bitcast.60, pred[]{:T(512)} %and_reduce_fusion, bf16[3,3,256,128]{3,2,1,0:T(8,128)(2,1)S(1)} %reshape.1187, bf16[1,2,8,8,512]{4,3,2,1,0:T(8,128)(2,1)S(1)} %copy-done), kind=kOutput, calls=%fused_computation.28 | convolution fusion | flops 33816576 | bytes 1245193 | tf_op jit(solution)/shard_map/nabjc,kc->nabjk/dot_general | solution.py:136
  29.0 2.9 %scatter-add.66 = f32[2,10,10,4,256]{4,2,1,0,3:T(8,128)S(1)} dynamic-update-slice(f32[2,10,10,4,256]{4,2,1,0,3:T(8,128)S(1)} %scatter-add.65, f32[2,8,8,4,256]{4,2,1,0,3:T(8,128)S(1)} %fusion.9, s32[]{:T(128)} %constant.794.clone.1, s32[]{:T(128)} %bitcast.59, s32[]{:T(128)} %bitcast.60, s32[]{:T(128)} %constant.794.clone.1, s32[]{:T(128)} %constant.794.clone.1) | dynamic-update-slice | bytes 1048580 | tf_op jit(solution)/shard_map/scatter-add | solution.py:144
  32.4 1.5 scatter-add.70
  34.2 1.5 scatter-add.71
  36.2 1.5 scatter-add.75
  38.0 1.5 scatter-add.76
  41.7 3.1 %scatter-add.85 = f32[2,10,10,512]{3,2,1,0:T(8,128)S(1)} dynamic-update-slice(f32[2,10,10,512]{3,2,1,0:T(8,128)S(1)} %slice.1260, f32[2,10,10,64]{3,2,1,0:T(8,128)S(1)} %get-tuple-element.368, s32[]{:T(128)} %constant.794.clone.1, s32[]{:T(128)} %constant.794.clone.1, s32[]{:T(128)} %constant.794.clone.1, s32[]{:T(128)} %constant.811.clone.1) | dynamic-update-slice | bytes 102404 | tf_op jit(solution)/shard_map/scatter-add | solution.py:155
  45.6 1.3 collective-permute-start.4
  46.9 4.5 %collective-permute-start.5 = (bf16[2,10,512]{2,0,1:T(2,128)(2,1)S(1)}, bf16[2,10,512]{2,0,1:T(2,128)(2,1)S(1)}, u32[]{:S(2)}, u32[]{:S(2)}) collective-permute-start(bf16[2,10,512]{2,0,1:T(2,128)(2,1)S(1)} %bitcast.421), channel_id=1, source_target_pairs={{0,2},{2,4},{4,6},{6,8},{8,10},{10,12},{12,14},{1,3},{3,5},{5,7},{... | collective-permute-start | bytes 61448 | tf_op jit(solution)/shard_map/ppermute | solution.py:13
  53.1 1.3 collective-permute-start.3
  54.4 4.9 %collective-permute-start.2 = (bf16[2,10,512]{2,1,0:T(8,128)(2,1)S(1)}, bf16[2,10,512]{2,1,0:T(8,128)(2,1)S(1)}, u32[]{:S(2)}, u32[]{:S(2)}) collective-permute-start(bf16[2,10,512]{2,1,0:T(8,128)(2,1)S(1)} %copy.364), channel_id=1, source_target_pairs={{0,2},{2,4},{4,6},{6,8},{8,10},{10,12},{12,14},{1,3},{3,5},{5,7},{... | collective-permute-start | bytes 61448 | tf_op jit(solution)/shard_map/ppermute | solution.py:13
  61.4 5.4 %collective-permute-start.7 = (bf16[2,8,512]{2,1,0:T(8,128)(2,1)S(1)}, bf16[2,8,512]{2,1,0:T(8,128)(2,1)S(1)}, u32[]{:S(2)}, u32[]{:S(2)}) collective-permute-start(bf16[2,8,512]{2,1,0:T(8,128)(2,1)S(1)} %get-tuple-element.365), channel_id=1, source_target_pairs={{0,8},{2,10},{4,12},{6,14},{1,9},{3,11},{5,13},{7,15},{16,24},{18,... | collective-permute-start | bytes 49160 | tf_op jit(solution)/shard_map/ppermute | solution.py:13
  66.9 1.5 collective-permute-start.6
  72.3 1.5 fusion.129
  85.4 2.7 %reshape.1202 = f32[3,3,4,64,2,64]{5,4,3,2,1,0:T(2,128)S(1)} reshape(f32[9,256,128]{2,1,0:T(8,128)} %fusion.13) | data formatting | bytes 2359296 | tf_op jit(solution)/shard_map/reshape | solution.py:120
  88.0 1.9 fusion.128
  93.3 19.9 %all-reduce.6.cloned.1.call-done = f32[3,3,3,64,64]{4,3,2,1,0:T(8,128)} async-done(((f32[3,3,3,64,64]{4,3,2,1,0:T(8,128)}), f32[3,3,3,64,64]{4,3,2,1,0:T(8,128)}) %all-reduce.6.cloned.1.call-update) | async-done | bytes 442384 | tf_op jit(solution)/shard_map/psum | solution.py:130
  114.3 1.7 fusion.12
  116.1 77.6 %all-reduce.8.cloned.1.call-done = f32[3,3,3,64,64]{4,3,2,1,0:T(8,128)} async-done(((f32[3,3,3,64,64]{4,3,2,1,0:T(8,128)}), f32[3,3,3,64,64]{4,3,2,1,0:T(8,128)}) %all-reduce.8.cloned.1.call-update) | async-done | bytes 442384 | tf_op jit(solution)/shard_map/psum | solution.py:130
  193.7 2.2 %broadcast_multiply_fusion = f32[3,3,3,64,64]{4,3,2,1,0:T(8,128)} fusion(f32[3,3,3,64,64]{4,3,2,1,0:T(8,128)} %all-reduce.8.cloned.1.call-done), kind=kLoop, calls=%fused_computation.62 | loop fusion | flops 110592 | bytes 884736 | tf_op jit(solution)/shard_map/mul | solution.py:130
  (177 shorter events, 35.3 us)
Async XLA Ops:
  7.2 14.9 %copy-start = (bf16[1,2,8,8,512]{4,3,2,1,0:T(8,128)(2,1)S(1)}, bf16[1,2,8,8,512]{4,3,2,1,0:T(8,128)(2,1)}, u32[]{:S(2)}) copy-start(bf16[1,2,8,8,512]{4,3,2,1,0:T(8,128)(2,1)} %param.67) | copy-start | bytes 393220
  7.2 12.2 %copy-start.2 = (bf16[3,3,3,64,64]{4,3,2,1,0:T(8,128)(2,1)S(1)}, bf16[3,3,3,64,64]{4,3,2,1,0:T(8,128)(2,1)}, u32[]{:S(2)}) copy-start(bf16[3,3,3,64,64]{4,3,2,1,0:T(8,128)(2,1)} %param.68) | copy-start | bytes 663556
  7.2 106.0 %all-reduce.6.cloned.1.call-start = ((), (), s32[]{:S(2)}) async-start(), calls=%async_computation | async-start | bytes 1769472 | tf_op jit(solution)/shard_map/psum | solution.py:130
  8.0 43.7 %collective-permute-start = (bf16[2,8,512]{2,1,0:T(8,128)(2,1)S(1)}, bf16[2,8,512]{2,1,0:T(8,128)(2,1)S(1)}, u32[]{:S(2)}, u32[]{:S(2)}) collective-permute-start(bf16[2,8,512]{2,1,0:T(8,128)(2,1)S(1)} %get-tuple-element.377), channel_id=1, source_target_pairs={{0,8},{2,10},{4,12},{6,14},{1,9},{3,11},{5,13},{7,15},{16,24},{18,... | collective-permute-start | bytes 49160 | tf_op jit(solution)/shard_map/ppermute | solution.py:13
  14.0 38.3 %collective-permute-start.1 = (bf16[2,8,512]{2,1,0:T(8,128)(2,1)S(1)}, bf16[2,8,512]{2,1,0:T(8,128)(2,1)S(1)}, u32[]{:S(2)}, u32[]{:S(2)}) collective-permute-start(bf16[2,8,512]{2,1,0:T(8,128)(2,1)S(1)} %get-tuple-element.378), channel_id=1, source_target_pairs={{8,0},{10,2},{12,4},{14,6},{9,1},{11,3},{13,5},{15,7},{24,16},{26,... | collective-permute-start | bytes 49160 | tf_op jit(solution)/shard_map/ppermute | solution.py:13
  20.7 0.7 copy-start.12
  21.4 53.2 %copy-start.1 = (bf16[3,3,256,128]{3,2,1,0:T(8,128)(2,1)}, bf16[3,3,256,128]{3,2,1,0:T(8,128)(2,1)S(1)}, u32[]{:S(2)}) copy-start(bf16[3,3,256,128]{3,2,1,0:T(8,128)(2,1)S(1)} %reshape.1187) | copy-start | bytes 1769476
  44.8 8.1 %copy-start.3 = (bf16[1,2,8,8,512]{4,3,2,1,0:T(8,128)(2,1)S(1)}, bf16[1,2,8,8,512]{4,3,2,1,0:T(8,128)(2,1)}, u32[]{:S(2)}) copy-start(bf16[1,2,8,8,512]{4,3,2,1,0:T(8,128)(2,1)} %param.66) | copy-start | bytes 393220
  45.6 13.9 %collective-permute-start.4 = (bf16[2,10,512]{2,0,1:T(2,128)(2,1)S(1)}, bf16[2,10,512]{2,0,1:T(2,128)(2,1)S(1)}, u32[]{:S(2)}, u32[]{:S(2)}) collective-permute-start(bf16[2,10,512]{2,0,1:T(2,128)(2,1)S(1)} %bitcast.420), channel_id=1, source_target_pairs={{2,0},{4,2},{6,4},{8,6},{10,8},{12,10},{14,12},{3,1},{5,3},{7,5},{... | collective-permute-start | bytes 61448 | tf_op jit(solution)/shard_map/ppermute | solution.py:13
  46.9 12.5 %collective-permute-start.5 = (bf16[2,10,512]{2,0,1:T(2,128)(2,1)S(1)}, bf16[2,10,512]{2,0,1:T(2,128)(2,1)S(1)}, u32[]{:S(2)}, u32[]{:S(2)}) collective-permute-start(bf16[2,10,512]{2,0,1:T(2,128)(2,1)S(1)} %bitcast.421), channel_id=1, source_target_pairs={{0,2},{2,4},{4,6},{6,8},{8,10},{10,12},{12,14},{1,3},{3,5},{5,7},{... | collective-permute-start | bytes 61448 | tf_op jit(solution)/shard_map/ppermute | solution.py:13
  53.1 15.2 %collective-permute-start.3 = (bf16[2,10,512]{2,1,0:T(8,128)(2,1)S(1)}, bf16[2,10,512]{2,1,0:T(8,128)(2,1)S(1)}, u32[]{:S(2)}, u32[]{:S(2)}) collective-permute-start(bf16[2,10,512]{2,1,0:T(8,128)(2,1)S(1)} %copy.368), channel_id=1, source_target_pairs={{2,0},{4,2},{6,4},{8,6},{10,8},{12,10},{14,12},{3,1},{5,3},{7,5},{... | collective-permute-start | bytes 61448 | tf_op jit(solution)/shard_map/ppermute | solution.py:13
  54.4 14.7 %collective-permute-start.2 = (bf16[2,10,512]{2,1,0:T(8,128)(2,1)S(1)}, bf16[2,10,512]{2,1,0:T(8,128)(2,1)S(1)}, u32[]{:S(2)}, u32[]{:S(2)}) collective-permute-start(bf16[2,10,512]{2,1,0:T(8,128)(2,1)S(1)} %copy.364), channel_id=1, source_target_pairs={{0,2},{2,4},{4,6},{6,8},{8,10},{10,12},{12,14},{1,3},{3,5},{5,7},{... | collective-permute-start | bytes 61448 | tf_op jit(solution)/shard_map/ppermute | solution.py:13
  61.4 13.4 %collective-permute-start.7 = (bf16[2,8,512]{2,1,0:T(8,128)(2,1)S(1)}, bf16[2,8,512]{2,1,0:T(8,128)(2,1)S(1)}, u32[]{:S(2)}, u32[]{:S(2)}) collective-permute-start(bf16[2,8,512]{2,1,0:T(8,128)(2,1)S(1)} %get-tuple-element.365), channel_id=1, source_target_pairs={{0,8},{2,10},{4,12},{6,14},{1,9},{3,11},{5,13},{7,15},{16,24},{18,... | collective-permute-start | bytes 49160 | tf_op jit(solution)/shard_map/ppermute | solution.py:13
  66.9 8.5 %collective-permute-start.6 = (bf16[2,8,512]{2,1,0:T(8,128)(2,1)S(1)}, bf16[2,8,512]{2,1,0:T(8,128)(2,1)S(1)}, u32[]{:S(2)}, u32[]{:S(2)}) collective-permute-start(bf16[2,8,512]{2,1,0:T(8,128)(2,1)S(1)} %get-tuple-element.366), channel_id=1, source_target_pairs={{8,0},{10,2},{12,4},{14,6},{9,1},{11,3},{13,5},{15,7},{24,16},{26,... | collective-permute-start | bytes 49160 | tf_op jit(solution)/shard_map/ppermute | solution.py:13
  74.5 2.3 %copy-start.11 = (bf16[2,8,8,4,256]{4,2,3,1,0:T(8,128)(2,1)S(1)}, bf16[2,8,8,4,256]{4,2,3,1,0:T(8,128)(2,1)}, u32[]{:S(2)}) copy-start(bf16[2,8,8,4,256]{4,2,3,1,0:T(8,128)(2,1)} %get-tuple-element.360) | copy-start | bytes 786436
  76.9 1.0 copy-start.10
  77.8 0.9 copy-start.9
  78.8 0.9 copy-start.8
  79.7 0.9 copy-start.7
  80.7 0.9 copy-start.6
  81.6 0.9 copy-start.5
  82.6 0.9 copy-start.4
  91.1 102.6 %all-reduce.8.cloned.1.call-start = ((), (), s32[]{:S(2)}) async-start(), calls=%async_computation.1 | async-start | bytes 1769472 | tf_op jit(solution)/shard_map/psum | solution.py:130
Sparse Core Ops, SparseCore 0:
  91.2 21.9 all-reduce.5
  116.7 76.9 all-reduce.7
